TPU v7x, 128 devices: a whole 4x4x4 slice. The times are simulated.
128 devices in a mesh: span: 32 (over x, z, y_lo), ctx: 4 (over y_hi, core).
Axes of the slice: x: 4, y: 4 (y_hi: 2, y_lo: 2; y = y_hi * 2 + y_lo), z: 4, core: 2. Of those that a mesh axis runs over, the one named last changes fastest.
Arguments:
- queries: bfloat16 [16384, 3072], P(('span', 'ctx')), may hold values from -64 to 64
- keys: bfloat16 [16384, 512], P(('span', 'ctx')), may hold values from -16 to 16
- values: bfloat16 [16384, 512], P(('span', 'ctx')), may hold values from -6 to 6
- temps: float32 [8, 24], replicated, may hold values from 0.5 to 2
- levels: int32 [32], replicated, may hold values from 0 to 7
- ctx_list: int32 [32, 4], replicated, may hold values from -1 to 30, as said below
- counts: int32 [32], replicated, may hold values from 256 to 512
Outputs:
- attended: bfloat16 [16384, 3072], P(('span', 'ctx'))
Inputs may be any that keep to these rules, and one draw needn't show every extreme that they name: `ctx_list`: slot 0 of span c's list is c - 1 (-1 for span 0). Slot 1, when used, is span 0. The other slots hold distinct spans below c - 1, used slots first, then -1. The list of span 32 - 1 has no -1.
All inputs are finite; a program needn't handle non-finite values.
Results may differ from a plain program's by a relative error of at most 0.0041.
Values may be sent and summed in bfloat16 or wider, within the bound.
A program may use at most 128 MiB of HBM per device.

v0:
```python
import math
import jax
import jax.numpy as jnp
from jax import lax
from jax.sharding import PartitionSpec as P

HQ = 24
KVH = 4
HD = 128


def slot_scores(query_group, key_slot, scale_group):
    scores = jnp.einsum("rgd,kd->grk", query_group, key_slot, preferred_element_type=jnp.float32)
    return scores * scale_group[:, None, None]


def row_maxima(query_rows, key_slots, mask, scale):
    group_size = HQ // KVH
    row_count = query_rows.shape[0]
    query_heads = query_rows.reshape(row_count, HQ, HD)
    maxima = []
    for kv_head in range(KVH):
        lower = kv_head * group_size
        query_group = query_heads[:, lower : lower + group_size]
        highest = jnp.full((group_size, row_count), -1e30, jnp.float32)
        for slot_index in range(key_slots.shape[0]):
            scores = slot_scores(
                query_group,
                key_slots[slot_index][:, kv_head * HD : (kv_head + 1) * HD],
                scale[lower : lower + group_size],
            )
            scores = jnp.where(mask[slot_index][None, None, :], scores, -1e30)
            highest = jnp.maximum(highest, jnp.max(scores, axis=-1))
        maxima.append(highest)
    return jnp.concatenate(maxima, axis=0)


def weighted_sums(query_rows, key_slots, value_slots, mask, scale, maxima):
    group_size = HQ // KVH
    row_count = query_rows.shape[0]
    query_heads = query_rows.reshape(row_count, HQ, HD)
    sums_list = []
    totals_list = []
    for kv_head in range(KVH):
        lower = kv_head * group_size
        query_group = query_heads[:, lower : lower + group_size]
        highest = maxima[lower : lower + group_size]
        accum = jnp.zeros((row_count, group_size, HD), jnp.float32)
        totals = jnp.zeros((group_size, row_count), jnp.float32)
        for slot_index in range(key_slots.shape[0]):
            scores = slot_scores(
                query_group,
                key_slots[slot_index][:, kv_head * HD : (kv_head + 1) * HD],
                scale[lower : lower + group_size],
            )
            keep = mask[slot_index][None, None, :]
            scores = jnp.where(keep, scores, -1e30)
            weights = jnp.where(keep, jnp.exp(scores - highest[:, :, None]), 0.0)
            totals = totals + jnp.sum(weights, axis=-1)
            value_group = value_slots[slot_index][:, kv_head * HD : (kv_head + 1) * HD]
            accum = accum + jnp.einsum(
                "grk,kd->rgd",
                weights.astype(jnp.bfloat16),
                value_group,
                preferred_element_type=jnp.float32,
            )
        sums_list.append(accum)
        totals_list.append(totals)
    sums = jnp.concatenate(sums_list, axis=1).reshape(row_count, HQ * HD)
    totals = jnp.transpose(jnp.concatenate(totals_list, axis=0))
    return (sums, totals)


def finish(sums, totals):
    row_count = sums.shape[0]
    result = sums.reshape(row_count, HQ, HD) / totals[:, :, None]
    return result.reshape(row_count, HQ * HD).astype(jnp.bfloat16)


def per_device(queries, keys, values, temps, levels, ctx_list, counts):
    span_index = lax.axis_index("span")
    tok_rows = keys.shape[0]
    width = keys.shape[1]
    wanted = lax.dynamic_index_in_dim(ctx_list, span_index, 0, keepdims=False)
    empty = jnp.zeros((wanted.shape[0], tok_rows, width), keys.dtype)
    piece_keys = lax.all_gather(keys, "span", axis=0, tiled=True)
    piece_values = lax.all_gather(values, "span", axis=0, tiled=True)
    length = piece_keys.shape[0]
    new_keys = []
    new_values = []
    for slot_index in range(wanted.shape[0]):
        source = wanted[slot_index]
        offset = source * tok_rows
        inside = (source >= 0) & (offset >= 0) & (offset + tok_rows <= length)
        begin = jnp.clip(offset, 0, length - tok_rows)
        slab_keys = lax.dynamic_slice_in_dim(piece_keys, begin, tok_rows, 0)
        slab_values = lax.dynamic_slice_in_dim(piece_values, begin, tok_rows, 0)
        new_keys.append(lax.select(inside, slab_keys, empty[slot_index]))
        new_values.append(lax.select(inside, slab_values, empty[slot_index]))
    context_keys = jnp.stack(new_keys)
    context_values = jnp.stack(new_values)
    slot_keys = jnp.concatenate([keys[None], context_keys], axis=0)
    slot_values = jnp.concatenate([values[None], context_values], axis=0)
    span_ids = jnp.concatenate([jnp.reshape(span_index, (1,)), wanted])
    valid_span = span_ids >= 0
    lengths = counts[jnp.maximum(span_ids, 0)]
    level = lax.dynamic_index_in_dim(levels, span_index, 0, keepdims=False)
    scale = lax.dynamic_index_in_dim(temps, level, 0, keepdims=False) / math.sqrt(HD)
    all_keys, all_values = (
        lax.all_gather(slot_keys, "ctx", axis=1, tiled=True),
        lax.all_gather(slot_values, "ctx", axis=1, tiled=True),
    )
    positions = jnp.arange(all_keys.shape[1], dtype=jnp.int32)
    mask = valid_span[:, None] & (positions[None, :] < lengths[:, None])
    maxima = row_maxima(queries, all_keys, mask, scale)
    sums, totals = weighted_sums(queries, all_keys, all_values, mask, scale, maxima)
    return finish(sums, totals)


def solution(mesh):
    return jax.shard_map(
        per_device,
        mesh=mesh,
        in_specs=(
            P(("span", "ctx"), None),
            P(("span", "ctx"), None),
            P(("span", "ctx"), None),
            P(),
            P(),
            P(),
            P(),
        ),
        out_specs=P(("span", "ctx"), None),
        check_vma=False,
    )
```

profile of v0, /device:TPU:1, one launch (start us, length us, event | category | flops | bytes accessed | tf_op | source)
XLA Modules:
  0.0 432.0 jit_solution(16926289602360051760)
XLA Ops:
  6.5 0.7 all-gather.9.cloned.1.call-update
  8.1 0.9 fusion.212
  14.5 0.9 bitcast_dynamic-update-slice_fusion.4
  15.4 0.9 bitcast_dynamic-update-slice_fusion.9
  16.3 133.3 %all-gather.9.cloned.1.call-done = bf16[4096,512]{1,0:T(8,128)(2,1)} async-done(((bf16[128,512]{1,0:T(8,128)(2,1)}), bf16[4096,512]{1,0:T(8,128)(2,1)}) %all-gather.9.cloned.1.call-update) | async-done | bytes 4194320 | tf_op jit(solution)/shard_map/all_gather | solution.py:86
  149.6 159.8 %all-gather.5.cloned.1.call-done = bf16[4096,512]{1,0:T(8,128)(2,1)} async-done(((bf16[128,512]{1,0:T(8,128)(2,1)}), bf16[4096,512]{1,0:T(8,128)(2,1)}) %all-gather.5.cloned.1.call-update) | async-done | bytes 4194320 | tf_op jit(solution)/shard_map/all_gather | solution.py:87
  309.5 1.1 bitcast_dynamic-update-slice_fusion.3
  310.5 1.0 bitcast_dynamic-update-slice_fusion.2
  311.5 1.0 bitcast_dynamic-update-slice_fusion.1
  312.5 1.0 bitcast_dynamic-update-slice_fusion
  313.4 0.8 copy-done.20
  318.3 0.7 fusion.190
  319.2 1.0 bitcast_dynamic-update-slice_fusion.7
  320.2 1.0 bitcast_dynamic-update-slice_fusion.6
  321.1 1.0 bitcast_dynamic-update-slice_fusion.5
  322.1 0.8 copy-done.21
  322.9 42.3 %all-gather.11.cloned.1.call-done = bf16[5,512,512]{2,1,0:T(8,128)(2,1)} async-done(((bf16[5,128,512]{2,1,0:T(8,128)(2,1)}), bf16[5,512,512]{2,1,0:T(8,128)(2,1)}) %all-gather.11.cloned.1.call-update) | async-done | bytes 2621456 | tf_op jit(solution)/shard_map/all_gather | solution.py:110
  365.3 1.9 slice_bitcast_fusion.7
  367.2 1.5 bitcast_reduce_fusion.19
  369.1 1.5 bitcast_reduce_fusion.18
  370.6 1.5 bitcast_reduce_fusion.17
  372.1 1.5 bitcast_reduce_fusion.16
  373.7 1.6 bitcast_reduce_fusion.15
  375.3 1.5 bitcast_reduce_fusion.13
  376.8 1.6 bitcast_reduce_fusion.12
  378.3 1.6 bitcast_reduce_fusion.11
  379.9 1.6 bitcast_reduce_fusion.10
  381.5 1.5 bitcast_reduce_fusion.9
  383.0 1.5 bitcast_reduce_fusion.8
  384.6 1.5 bitcast_reduce_fusion.4
  386.1 1.6 bitcast_reduce_fusion.3
  387.6 1.5 bitcast_reduce_fusion.7
  389.2 1.5 bitcast_reduce_fusion.2
  390.7 1.5 bitcast_reduce_fusion.6
  392.2 1.5 bitcast_reduce_fusion.1
  393.7 1.6 bitcast_reduce_fusion
  395.3 1.5 bitcast_reduce_fusion.5
  396.8 2.1 slice_bitcast_fusion
  399.5 0.8 copy-done.3
  401.5 0.8 copy-done.16
  403.5 0.7 copy-done.17
  407.2 3.4 fusion.73
  412.0 0.9 copy-done.4
  414.0 0.8 copy-done.6
  416.0 0.8 copy-done.1
  417.9 0.7 copy-done.9
  419.7 3.4 fusion.63
  424.3 1.2 copy.94
  (88 shorter events, 16.5 us)
Async XLA Ops:
  6.5 311.1 %copy-start = (s32[32]{0:T(128)S(1)}, s32[32]{0:T(128)}, u32[]{:S(2)}) copy-start(s32[32]{0:T(128)} %param.13) | copy-start | bytes 388
  6.5 307.8 %copy-start.23 = (s32[32]{0:T(128)S(1)}, s32[32]{0:T(128)}, u32[]{:S(2)}) copy-start(s32[32]{0:T(128)} %param.11) | copy-start | bytes 388
  6.5 309.9 %copy-start.22 = (bf16[128,3072]{1,0:T(8,128)(2,1)S(1)}, bf16[128,3072]{1,0:T(8,128)(2,1)}, u32[]{:S(2)}) copy-start(bf16[128,3072]{1,0:T(8,128)(2,1)} %param.7) | copy-start | bytes 2359300
  6.5 143.1 %all-gather.9.cloned.1.call-start = ((), (), s32[]{:S(2)}) async-start(), calls=%async_computation.2 | async-start | bytes 4325376 | tf_op jit(solution)/shard_map/all_gather | solution.py:86
  7.3 302.2 %all-gather.5.cloned.1.call-start = ((), (), s32[]{:S(2)}) async-start(), calls=%async_computation | async-start | bytes 4325376 | tf_op jit(solution)/shard_map/all_gather | solution.py:87
  8.0 357.2 %all-gather.11.cloned.1.call-start = ((), (), s32[]{:S(2)}) async-start(), calls=%async_computation.3 | async-start | bytes 3276800 | tf_op jit(solution)/shard_map/all_gather | solution.py:110
  313.4 0.8 copy-start.20
  314.3 82.6 %all-gather.7.cloned.1.call-start = ((), (), s32[]{:S(2)}) async-start(), calls=%async_computation.1 | async-start | bytes 3276800 | tf_op jit(solution)/shard_map/all_gather | solution.py:111
  322.1 0.8 copy-start.21
  396.8 2.2 copy-start.2
  398.9 1.4 copy-start.3
  399.5 1.5 copy-start.12
  400.8 1.5 copy-start.16
  401.5 1.5 copy-start.13
  402.7 1.5 copy-start.17
  403.5 1.5 copy-start.15
  404.7 1.5 copy-start.19
  405.0 1.6 copy-start.18
  405.5 1.7 copy-start.14
  411.5 1.4 copy-start.4
  412.0 1.5 copy-start.5
  413.4 1.4 copy-start.6
  414.0 1.5 copy-start.7
  415.3 1.5 copy-start.1
  415.9 1.5 copy-start.8
  417.2 1.5 copy-start.9
  417.5 1.6 copy-start.11
  417.9 1.8 copy-start.10
Sparse Core Ops, SparseCore 0:
  9.0 140.5 all-gather.8
  151.3 158.1 all-gather.4
  314.4 50.8 all-gather.10
  366.8 28.9 all-gather.6
where the time goes:
time: 433 us; the launch traced here: 432 us
  waiting for transfers between devices  337 us (78%)
  matrix products  38.6 us (9%)
  local copies, waits for them, and re-layouts  20.9 us (5%)
  between operations  20.7 us (5%)
  other arithmetic  14.8 us (3%)
    all_gather x1, waiting for transfers between devices, per_device(): piece_values = lax.all_gather(values, 'span', axis=0, tiled=True)  160 us
    all_gather x1, waiting for transfers between devices, per_device(): piece_keys = lax.all_gather(keys, 'span', axis=0, tiled=True)  133 us
    all_gather x1, waiting for transfers between devices, per_device(): lax.all_gather(slot_keys, 'ctx', axis=1, tiled=True)  42.3 us
    dot_general x20, matrix products, slot_scores(): jnp.einsum('rgd,kd->grk', query_group, key_slot, preferred_element_type=j...  29.6 us
    unnamed x51, local copies, waits for them, and re-layouts  12.9 us
    dot_general x20, matrix products, weighted_sums(): jnp.einsum('grk,kd->rgd', weights.astype(jnp.bfloat16), value_group, pref...  8.94 us
  transfers between devices with their start and end apart: 4, of which 3 were waited for; matrix products, arithmetic and copies ran while one was open for 9% of the time, Pallas kernels for 0%

commit v1 on v0

--- a/solution.py
+++ b/solution.py
@@ -84,7 +84,15 @@
     wanted = lax.dynamic_index_in_dim(ctx_list, span_index, 0, keepdims=False)
     empty = jnp.zeros((wanted.shape[0], tok_rows, width), keys.dtype)
     piece_keys = lax.all_gather(keys, "span", axis=0, tiled=True)
-    piece_values = lax.all_gather(values, "span", axis=0, tiled=True)
+    piece_values = jnp.concatenate(
+        lax.all_to_all(
+            jnp.stack(lax.axis_size("span") * [values], axis=0),
+            axis_name="span",
+            split_axis=0,
+            concat_axis=0,
+        ),
+        axis=0,
+    )
     length = piece_keys.shape[0]
     new_keys = []
     new_values = []

time: 433 us -> 314 us (0.73)
  waiting for transfers between devices: 337 us -> 207 us
  starting transfers between devices: 0.12 us -> 10.1 us
    all_gather x1 -> x0, waiting for transfers between devices: 160 us -> none  [per_device(): piece_values = lax.all_gather(values, 'span', axis=0, tiled=True)]
    all_to_all x0 -> x1, waiting for transfers between devices: none -> 51.1 us  [per_device(): lax.all_to_all(jnp.stack(lax.axis_size('span') * [values], axis=0), axis_...]
    all_gather x1, waiting for transfers between devices: 133 us -> 117 us  [per_device(): piece_keys = lax.all_gather(keys, 'span', axis=0, tiled=True)]
    all_to_all x0 -> x1, starting transfers between devices: none -> 9.99 us  [per_device(): lax.all_to_all(jnp.stack(lax.axis_size('span') * [values], axis=0), axis_...]
    all_gather x1, waiting for transfers between devices: 42.3 us -> 38 us  [per_device(): lax.all_gather(slot_keys, 'ctx', axis=1, tiled=True)]
    unnamed x51 -> x59, local copies, waits for them, and re-layouts: 12.9 us -> 11.1 us
  transfers between devices with their start and end apart: 4 -> 4, of which waited for: 3 -> 3; matrix products, arithmetic and copies ran while one was open for 9% -> 13% of each run, Pallas kernels for 0% -> 0%
where the time goes in v1:
time: 314 us; the launch traced here: 313 us
  waiting for transfers between devices  207 us (66%)
  matrix products  38.6 us (12%)
  local copies, waits for them, and re-layouts  21.9 us (7%)
  between operations  21.1 us (7%)
  other arithmetic  14.9 us (5%)
  starting transfers between devices  10.1 us (3%)
    all_gather x1, waiting for transfers between devices, per_device(): piece_keys = lax.all_gather(keys, 'span', axis=0, tiled=True)  117 us
    all_to_all x1, waiting for transfers between devices, per_device(): lax.all_to_all(jnp.stack(lax.axis_size('span') * [values], axis=0), axis_...  51.1 us
    all_gather x1, waiting for transfers between devices, per_device(): lax.all_gather(slot_keys, 'ctx', axis=1, tiled=True)  38 us
    dot_general x20, matrix products, slot_scores(): jnp.einsum('rgd,kd->grk', query_group, key_slot, preferred_element_type=j...  29.6 us
    unnamed x59, local copies, waits for them, and re-layouts  11.1 us
    all_to_all x1, starting transfers between devices, per_device(): lax.all_to_all(jnp.stack(lax.axis_size('span') * [values], axis=0), axis_...  9.99 us
    dot_general x20, matrix products, weighted_sums(): jnp.einsum('grk,kd->rgd', weights.astype(jnp.bfloat16), value_group, pref...  8.96 us
    reduce_sum x2, other arithmetic, weighted_sums(): totals = totals + jnp.sum(weights, axis=-1)  6.85 us
  transfers between devices with their start and end apart: 4, of which 3 were waited for; matrix products, arithmetic and copies ran while one was open for 13% of the time, Pallas kernels for 0%

profile of v1, /device:TPU:1, one launch (start us, length us, event | category | flops | bytes accessed | tf_op | source)
XLA Modules:
  0.0 313.2 jit_solution(7758841934015886435)
XLA Ops:
  6.5 0.7 all-gather.6.cloned.1.call-update
  7.3 3.4 %stack.18 = bf16[32,128,512]{2,1,0:T(8,128)(2,1)} broadcast(bf16[128,512]{1,0:T(8,128)(2,1)} %param.9), dimensions={1,2} | broadcast | bytes 4325376 | tf_op jit(solution)/shard_map/stack | solution.py:89
  10.6 10.0 %all-to-all-start = ((bf16[32,128,512]{2,1,0:T(8,128)(2,1)}), bf16[32,128,512]{2,1,0:T(8,128)(2,1)}, u32[]{:S(2)}, u32[]{:S(2)}) async-start(bf16[32,128,512]{2,1,0:T(8,128)(2,1)} %stack.18), calls=%async_computation | async-start | bytes 8388608 | tf_op jit(solution)/shard_map/all_to_all | solution.py:88
  26.9 51.1 %all-to-all-done = bf16[32,128,512]{2,1,0:T(8,128)(2,1)} async-done(((bf16[32,128,512]{2,1,0:T(8,128)(2,1)}), bf16[32,128,512]{2,1,0:T(8,128)(2,1)}, u32[]{:S(2)}, u32[]{:S(2)}) %all-to-all-start) | async-done | bytes 4194336 | tf_op jit(solution)/shard_map/all_to_all | solution.py:88
  78.0 116.9 %all-gather.6.cloned.1.call-done = bf16[4096,512]{1,0:T(8,128)(2,1)} async-done(((bf16[128,512]{1,0:T(8,128)(2,1)}), bf16[4096,512]{1,0:T(8,128)(2,1)}) %all-gather.6.cloned.1.call-update) | async-done | bytes 4194320 | tf_op jit(solution)/shard_map/all_gather | solution.py:86
  194.9 1.1 bitcast_dynamic-update-slice_fusion.3
  196.0 1.0 bitcast_dynamic-update-slice_fusion.2
  196.9 1.0 bitcast_dynamic-update-slice_fusion.1
  197.9 1.0 bitcast_dynamic-update-slice_fusion
  198.9 0.8 copy-done.21
  203.7 0.7 fusion.190
  204.6 1.0 bitcast_dynamic-update-slice_fusion.7
  205.6 1.0 bitcast_dynamic-update-slice_fusion.6
  206.5 1.0 bitcast_dynamic-update-slice_fusion.5
  207.5 0.8 copy-done.22
  208.4 38.0 %all-gather.8.cloned.1.call-done = bf16[5,512,512]{2,1,0:T(8,128)(2,1)} async-done(((bf16[5,128,512]{2,1,0:T(8,128)(2,1)}), bf16[5,512,512]{2,1,0:T(8,128)(2,1)}) %all-gather.8.cloned.1.call-update) | async-done | bytes 2621456 | tf_op jit(solution)/shard_map/all_gather | solution.py:118
  246.3 1.9 slice_bitcast_fusion.7
  248.3 1.5 bitcast_reduce_fusion.3
  249.8 1.5 bitcast_reduce_fusion.8
  251.3 1.6 bitcast_reduce_fusion
  252.9 1.6 bitcast_reduce_fusion.1
  254.5 1.5 bitcast_reduce_fusion.2
  256.0 1.6 bitcast_reduce_fusion.4
  257.7 1.6 bitcast_reduce_fusion.5
  259.2 1.6 bitcast_reduce_fusion.13
  260.8 1.5 bitcast_reduce_fusion.10
  262.3 1.5 bitcast_reduce_fusion.18
  263.8 1.5 bitcast_reduce_fusion.15
  265.3 1.5 bitcast_reduce_fusion.6
  266.8 1.5 bitcast_reduce_fusion.11
  268.3 1.5 bitcast_reduce_fusion.16
  269.9 1.5 bitcast_reduce_fusion.7
  271.8 1.5 bitcast_reduce_fusion.12
  273.3 1.6 bitcast_reduce_fusion.17
  274.9 1.5 bitcast_reduce_fusion.19
  276.4 1.5 bitcast_reduce_fusion.14
  277.9 2.1 slice_bitcast_fusion
  280.6 0.8 copy-done.4
  282.5 0.8 copy-done.18
  284.5 0.7 copy-done.20
  286.5 0.7 copy-done.19
  288.3 3.4 %fusion.73 = (f32[6,128]{1,0:T(8,128)S(1)}, f32[6,128]{1,0:T(8,128)S(1)}, f32[6,128]{1,0:T(8,128)S(1)}, f32[6,128]{1,0:T(8,128)S(1)}, f32[6,128]{1,0:T(8,128)S(1...) fusion(f32[512,128,6]{1,0,2:T(8,128)S(1)} %copy-done.14, ...), kind=kLoop, calls=%fused_computation.135 | loop fusion | flops 11788800 | bytes 15768064 | tf_op jit(solution)/shard_map/reduce_sum | solution.py:59
  293.1 0.9 copy-done.5
  295.1 0.8 copy-done.10
  297.1 0.8 copy-done.2
  299.1 0.7 copy-done.12
  300.8 3.4 %fusion.63 = (f32[6,128]{1,0:T(8,128)S(1)}, f32[6,128]{1,0:T(8,128)S(1)}, f32[6,128]{1,0:T(8,128)S(1)}, f32[6,128]{1,0:T(8,128)S(1)}, f32[6,128]{1,0:T(8,128)S(1...) fusion(f32[512,128,6]{1,0,2:T(8,128)S(1)} %copy-done.5, ...), kind=kLoop, calls=%fused_computation.125 | loop fusion | flops 11788800 | bytes 15768064 | tf_op jit(solution)/shard_map/reduce_sum | solution.py:59
  305.5 1.2 copy.94
  (96 shorter events, 15.3 us)
Async XLA Ops:
  6.5 196.5 %copy-start = (s32[32]{0:T(128)S(1)}, s32[32]{0:T(128)}, u32[]{:S(2)}) copy-start(s32[32]{0:T(128)} %param.13) | copy-start | bytes 388
  6.5 188.4 %all-gather.6.cloned.1.call-start = ((), (), s32[]{:S(2)}) async-start(), calls=%async_computation.2 | async-start | bytes 4325376 | tf_op jit(solution)/shard_map/all_gather | solution.py:86
  10.6 10.1 %copy-start.26 = (s32[32,4]{0,1:T(4,128)S(1)}, s32[32,4]{0,1:T(4,128)}, u32[]{:S(2)}) copy-start(s32[32,4]{0,1:T(4,128)} %param.12) | copy-start | bytes 1540
  10.6 16.2 %copy-start.25 = (bf16[128,512]{1,0:T(8,128)(2,1)S(1)}, bf16[128,512]{1,0:T(8,128)(2,1)}, u32[]{:S(2)}) copy-start(bf16[128,512]{1,0:T(8,128)(2,1)} %param.8) | copy-start | bytes 393220
  10.6 16.2 %copy-start.24 = (bf16[128,512]{1,0:T(8,128)(2,1)S(1)}, bf16[128,512]{1,0:T(8,128)(2,1)}, u32[]{:S(2)}) copy-start(bf16[128,512]{1,0:T(8,128)(2,1)} %param.9) | copy-start | bytes 393220
  10.6 67.3 %all-to-all-start = ((bf16[32,128,512]{2,1,0:T(8,128)(2,1)}), bf16[32,128,512]{2,1,0:T(8,128)(2,1)}, u32[]{:S(2)}, u32[]{:S(2)}) async-start(bf16[32,128,512]{2,1,0:T(8,128)(2,1)} %stack.18), calls=%async_computation | async-start | bytes 8388608 | tf_op jit(solution)/shard_map/all_to_all | solution.py:88
  20.6 179.1 %copy-start.27 = (s32[32]{0:T(128)S(1)}, s32[32]{0:T(128)}, u32[]{:S(2)}) copy-start(s32[32]{0:T(128)} %param.11) | copy-start | bytes 388
  20.6 181.2 %copy-start.23 = (bf16[128,3072]{1,0:T(8,128)(2,1)S(1)}, bf16[128,3072]{1,0:T(8,128)(2,1)}, u32[]{:S(2)}) copy-start(bf16[128,3072]{1,0:T(8,128)(2,1)} %param.7) | copy-start | bytes 2359300
  20.6 225.7 %all-gather.8.cloned.1.call-start = ((), (), s32[]{:S(2)}) async-start(), calls=%async_computation.3 | async-start | bytes 3276800 | tf_op jit(solution)/shard_map/all_gather | solution.py:118
  198.8 0.8 copy-start.21
  199.7 78.2 %all-gather.4.cloned.1.call-start = ((), (), s32[]{:S(2)}) async-start(), calls=%async_computation.1 | async-start | bytes 3276800 | tf_op jit(solution)/shard_map/all_gather | solution.py:119
  207.5 0.8 copy-start.22
  277.9 2.2 copy-start.3
  280.0 1.4 copy-start.4
  280.6 1.5 copy-start.14
  281.9 1.5 copy-start.18
  282.5 1.5 copy-start.16
  283.8 1.5 copy-start.20
  284.5 1.5 copy-start.15
  285.7 1.5 copy-start.19
  286.0 1.6 copy-start.17
  286.5 1.8 copy-start.13
  292.6 1.4 copy-start.5
  293.1 1.5 copy-start.11
  294.5 1.4 copy-start.10
  295.1 1.5 copy-start.7
  296.4 1.5 copy-start.2
  297.1 1.5 copy-start.8
  298.3 1.5 copy-start.12
  298.6 1.6 copy-start.9
  299.0 1.8 copy-start.6
  305.2 1.4 copy-start.1
Sparse Core Ops, SparseCore 0:
  9.0 185.8 all-gather.5
  199.8 46.4 all-gather.7
  248.0 29.0 all-gather.3
